TPU v7x, 32 devices: a whole 2x2x4 slice. The times are simulated.
32 devices in a mesh: grp: 2 (over y), row: 4 (over z), col: 4 (over x, core).
Axes of the slice: x: 2, y: 2, z: 4, core: 2. Of those that a mesh axis runs over, the one named last changes fastest.
Arguments:
- inputs: bfloat16 [256, 16384], P(('grp', 'row'), 'col'), parts along dimension 0, may hold values from -6 to 6
- output_gradient: bfloat16 [256, 16384], P(('grp', 'row'), 'col'), parts along dimension 0, may hold values from -6 to 6
- gate_preactivation: bfloat16 [256, 8192], P('grp', 'row'), parts along dimension 0, may hold values from -6 to 6
- up_preactivation: bfloat16 [256, 8192], P('grp', 'row'), parts along dimension 0, may hold values from -6 to 6
- gate_weight: bfloat16 [16384, 8192], P('col', 'row'), may hold values from -0.046875 to 0.046875
- up_weight: bfloat16 [16384, 8192], P('col', 'row'), may hold values from -0.046875 to 0.046875
- down_weight: bfloat16 [8192, 16384], P('row', 'col'), may hold values from -0.0625 to 0.0625
- up_adapter_entry: bfloat16 [16, 16384], P(None, 'col'), may hold values from -6 to 6
- up_adapter_exit: bfloat16 [16, 8192], P(None, 'row'), may hold values from -0.0032958984 to 0.0032958984
- down_adapter_entry: bfloat16 [16, 8192], P(None, 'row'), may hold values from -6 to 6
- down_adapter_exit: bfloat16 [16, 16384], P(None, 'col'), may hold values from -0.0023956299 to 0.0023956299
- up_adapter_activations: bfloat16 [16, 256], P(None, 'grp'), parts along dimension 1, may hold values from -0.29882812 to 0.29882812
- down_adapter_activations: bfloat16 [16, 256], P(None, 'grp'), parts along dimension 1, may hold values from -0.29882812 to 0.29882812
Outputs:
- grad_inputs: bfloat16 [256, 16384], P(('grp', 'row'), 'col'), parts along dimension 0
- up_entry_gradient: float32 [32, 16384], P('grp', 'col'), parts along dimension 0
- up_exit_gradient: float32 [32, 8192], P('grp', 'row'), parts along dimension 0
- down_entry_gradient: float32 [32, 8192], P('grp', 'row'), parts along dimension 0
- down_exit_gradient: float32 [32, 16384], P('grp', 'col'), parts along dimension 0
There are 2 independent parts, one for each index of `grp`. A program takes and returns all parts, laid end to end along the dimension named above; an argument that names none is the same for every part. Nothing has to cross between parts.
All inputs are finite; a program needn't handle non-finite values.
Results may differ from a plain program's by a relative error of at most 0.005.
Values may be sent and summed in bfloat16 or wider, within the bound.
No kernel may reach another device: no remote copies, remote signals or barrier semaphores. Data moves between devices by JAX's collectives and lax.ppermute only.
A program may use at most 128 MiB of HBM per device.

v0:
```python
import jax
import jax.numpy as jnp
from jax import lax
from jax.sharding import PartitionSpec as P

adapter_scale = 2.0


def contract_trailing(left, right):
    return lax.dot_general(
        left, right, (((1,), (1,)), ((), ())), preferred_element_type=jnp.float32
    )


def contract_leading(left, right, matmul_accuracy=None):
    return lax.dot_general(
        left,
        right,
        (((0,), (0,)), ((), ())),
        precision=matmul_accuracy,
        preferred_element_type=jnp.float32,
    )


def body(
    inputs,
    output_gradient,
    gate_preactivation,
    up_preactivation,
    gate_weight,
    up_weight,
    down_weight,
    up_adapter_entry,
    up_adapter_exit,
    down_adapter_entry,
    down_adapter_exit,
    up_adapter_activations,
    down_adapter_activations,
):
    highest_setting = lax.Precision.HIGHEST
    complete_gradient = lax.all_gather(output_gradient, "row", axis=0, tiled=True)
    down_piece = contract_trailing(complete_gradient, down_adapter_exit)
    hidden_piece = contract_trailing(complete_gradient, down_weight)
    hidden_piece = hidden_piece + adapter_scale * jnp.dot(
        down_piece, down_adapter_entry.astype(jnp.float32), precision=highest_setting
    )
    hidden_gradient, down_full = lax.psum((hidden_piece, down_piece), "col")
    gate_f = gate_preactivation.astype(jnp.float32)
    up_f = up_preactivation.astype(jnp.float32)
    sigmoid_gate = jax.nn.sigmoid(gate_f)
    hidden_state = (gate_f * sigmoid_gate * up_f).astype(jnp.bfloat16)
    gate_grad = (
        hidden_gradient * up_f * sigmoid_gate * (1.0 + gate_f * (1.0 - sigmoid_gate))
    ).astype(jnp.bfloat16)
    up_gradient = (hidden_gradient * gate_f * sigmoid_gate).astype(jnp.bfloat16)
    down_rounded_value = down_full.astype(jnp.bfloat16)
    upper_piece = contract_trailing(up_gradient, up_adapter_exit)
    input_piece = contract_trailing(gate_grad, gate_weight) + contract_trailing(
        up_gradient, up_weight
    )
    input_piece = input_piece + adapter_scale * jnp.dot(
        upper_piece, up_adapter_entry.astype(jnp.float32), precision=highest_setting
    )
    input_grad, upper_full = (
        lax.psum_scatter(input_piece, "row", scatter_dimension=0, tiled=True),
        lax.psum_scatter(upper_piece, "row", scatter_dimension=0, tiled=True),
    )
    up_entry_term = adapter_scale * contract_leading(
        upper_full, inputs.astype(jnp.float32), matmul_accuracy=highest_setting
    )
    up_entry_gradient = lax.psum(up_entry_term, "row")
    up_exit_gradient = adapter_scale * jnp.dot(
        up_adapter_activations, up_gradient, preferred_element_type=jnp.float32
    )
    down_entry_gradient = adapter_scale * contract_leading(down_rounded_value, hidden_state)
    down_exit_gradient = adapter_scale * jnp.dot(
        down_adapter_activations, complete_gradient, preferred_element_type=jnp.float32
    )
    return (
        input_grad.astype(jnp.bfloat16),
        up_entry_gradient,
        up_exit_gradient,
        down_entry_gradient,
        down_exit_gradient,
    )


def solution(mesh):
    placed = (
        P(("grp", "row"), "col"),
        P(("grp", "row"), "col"),
        P("grp", "row"),
        P("grp", "row"),
        P("col", "row"),
        P("col", "row"),
        P("row", "col"),
        P(None, "col"),
        P(None, "row"),
        P(None, "row"),
        P(None, "col"),
        P(None, "grp"),
        P(None, "grp"),
    )
    return jax.shard_map(
        body,
        mesh=mesh,
        in_specs=placed,
        out_specs=(
            P(("grp", "row"), "col"),
            P("grp", "col"),
            P("grp", "row"),
            P("grp", "row"),
            P("grp", "col"),
        ),
        check_vma=False,
    )
```

profile of v0, /device:TPU:0, one launch (start us, length us, event | category | flops | bytes accessed | tf_op | source)
XLA Modules:
  0.0 212.7 jit_solution(2744428697788110122)
XLA Ops:
  7.2 0.0 copy-start
  7.2 0.0 copy-start.5
  7.2 0.0 copy-start.3
  7.2 0.0 copy-start.6
  7.2 0.0 copy-start.7
  7.2 0.0 all-gather.2.cloned.1.call-start
  7.3 0.7 all-gather.2.cloned.1.call-update
  8.0 0.0 all-reduce.3.cloned.1.call-start
  8.0 32.3 %all-gather.2.cloned.1.call-done = bf16[128,4096]{1,0:T(8,128)(2,1)} async-done(((bf16[32,4096]{1,0:T(8,128)(2,1)}), bf16[128,4096]{1,0:T(8,128)(2,1)}) %all-gather.2.cloned.1.call-update) | async-done | bytes 1048592 | tf_op jit(solution)/shard_map/all_gather | solution.py:41
  40.3 1.6 fusion.21
  41.9 11.8 %fusion.20 = f32[128,2048]{1,0:T(8,128)S(1)} fusion(bf16[128,4096]{1,0:T(8,128)(2,1)} %all-gather.2.cloned.1.call-done, bf16[2048,4096]{1,0:T(8,128)(2,1)} %param.19), kind=kOutput, calls=%fused_computation.31 | convolution fusion | flops 2147483648 | bytes 18874368 | tf_op jit(solution)/shard_map/dot_general | solution.py:10
  53.7 0.0 copy-done.5
  53.7 1.6 fusion.1
  55.3 0.0 all-reduce.3.cloned.1.call-update
  55.3 0.0 reduce-scatter.7.cloned.1.call-start
  55.3 35.7 %all-reduce.3.cloned.1.call-done = f32[128,2048]{1,0:T(8,128)} async-done(((f32[128,2048]{1,0:T(8,128)}), f32[128,2048]{1,0:T(8,128)}) %all-reduce.3.cloned.1.call-update) | async-done | bytes 1048592 | tf_op jit(solution)/shard_map/psum | solution.py:47
  91.0 0.0 copy-done.3
  91.0 1.5 fusion.12
  92.5 0.0 copy-start.2
  92.5 0.8 copy-done.2
  93.3 0.0 copy-done.6
  93.3 0.2 fusion.22
  93.6 0.8 copy.18
  94.3 0.0 reduce-scatter.7.cloned.1.call-update
  94.4 0.0 copy-start.4
  94.4 0.2 reduce-scatter.5.cloned.1.call-start
  94.6 0.0 copy-done.7
  94.6 13.2 %fusion.13 = f32[128,4096]{1,0:T(8,128)} fusion(bf16[4096,2048]{1,0:T(8,128)(2,1)} %param.17, f32[128,2048]{1,0:T(8,128)} %all-reduce.3.cloned.1.call-done, bf16[128,2048]{1,0:T(8,128)(2,1)S(1)} %copy-done.7, bf16[128,2048]{1,0:T(8,128)(2,1)S(1)} %copy-done.3), kind=kOutput, calls=%fused_computation.26 | convolution fusion | flops 2150629376 | bytes 20971520 | tf_op jit(solution)/shard_map/dot_general | solution.py:10
  107.8 0.0 copy-start.1
  107.8 12.3 %convolution_add_fusion = f32[128,4096]{1,0:T(8,128)S(1)} fusion(f32[128,4096]{1,0:T(8,128)} %fusion.13, bf16[128,2048]{1,0:T(8,128)(2,1)} %copy-done.2, bf16[4096,2048]{1,0:T(8,128)(2,1)} %param.18), kind=kOutput, calls=%fused_computation.2 | convolution fusion | flops 2148007936 | bytes 21495808 | tf_op jit(solution)/shard_map/dot_general | solution.py:10
  120.1 0.0 copy-done.4
  120.1 2.4 %fusion = f32[128,4096]{1,0:T(8,128)} fusion(f32[128,4096]{1,0:T(8,128)S(1)} %convolution_add_fusion, f32[128,16]{0,1:T(8,128)S(1)} %fusion.22, bf16[16,4096]{1,0:T(8,128)(2,1)S(1)} %copy-done.4), kind=kOutput, calls=%fused_computation.1 | convolution fusion | flops 101711872 | bytes 4333568 | tf_op jit(solution)/shard_map/dot_general | solution.py:61
  122.5 0.0 reduce-scatter.5.cloned.1.call-update
  122.5 0.0 all-reduce.5.cloned.1.call-start
  122.6 6.0 %psum.23 = bf16[128,16]{0,1:T(8,128)(2,1)S(1)} all-reduce(f32[128,16]{0,1:T(8,128)S(1)} %fusion.21), channel_id=1, replica_groups=mesh['grp'=2,'row'=4,'col'=4] {'col'}, use_global_device_ids=true, to_apply=%region_4.0 | all-reduce | flops 2048 | bytes 12288 | tf_op jit(solution)/shard_map/psum | solution.py:47
  128.6 2.4 %convolution_multiply_fusion.5 = f32[16,2048]{1,0:T(8,128)} fusion(bf16[128,2048]{1,0:T(8,128)(2,1)} %param.16, bf16[128,2048]{1,0:T(8,128)(2,1)} %param.15, bf16[128,16]{0,1:T(8,128)(2,1)S(1)} %psum.23), kind=kOutput, calls=%fused_computation.9 | convolution fusion | flops 10518528 | bytes 1183744 | tf_op jit(solution)/shard_map/dot_general | solution.py:16
  131.0 0.0 reduce-scatter.7.cloned.1.call-done
  131.0 0.0 copy-done
  131.0 1.7 convolution_multiply_fusion.2
  132.7 0.0 all-reduce.5.cloned.1.call-update
  132.8 0.0 copy-done.1
  132.8 1.6 convolution_multiply_fusion.1
  134.4 1.9 fusion.2
  136.3 30.6 %reduce-scatter.5.cloned.1.call-done = f32[32,4096]{1,0:T(8,128)} async-done(((f32[128,4096]{1,0:T(8,128)}), f32[32,4096]{1,0:T(8,128)}) %reduce-scatter.5.cloned.1.call-update) | async-done | bytes 524304 | tf_op jit(solution)/shard_map/reduce_scatter | solution.py:65
  166.9 1.8 convert_element_type.28
  168.7 35.8 %all-reduce.5.cloned.1.call-done = f32[16,4096]{1,0:T(8,128)} async-done(((f32[16,4096]{1,0:T(8,128)}), f32[16,4096]{1,0:T(8,128)}) %all-reduce.5.cloned.1.call-update) | async-done | bytes 262160 | tf_op jit(solution)/shard_map/psum | solution.py:71
  204.5 1.7 copy.22
Async XLA Ops:
  7.2 123.8 %copy-start = (bf16[32,4096]{1,0:T(8,128)(2,1)S(1)}, bf16[32,4096]{1,0:T(8,128)(2,1)}, u32[]{:S(2)}) copy-start(bf16[32,4096]{1,0:T(8,128)(2,1)} %param.13) | copy-start | bytes 786436
  7.2 46.5 %copy-start.5 = (bf16[16,2048]{1,0:T(8,128)(2,1)S(1)}, bf16[16,2048]{1,0:T(8,128)(2,1)}, u32[]{:S(2)}) copy-start(bf16[16,2048]{1,0:T(8,128)(2,1)} %param.22) | copy-start | bytes 196612
  7.2 83.8 %copy-start.3 = (bf16[128,2048]{1,0:T(8,128)(2,1)S(1)}, bf16[128,2048]{1,0:T(8,128)(2,1)}, u32[]{:S(2)}) copy-start(bf16[128,2048]{1,0:T(8,128)(2,1)} %param.15) | copy-start | bytes 1572868
  7.2 86.1 %copy-start.6 = (bf16[16,2048]{1,0:T(8,128)(2,1)S(1)}, bf16[16,2048]{1,0:T(8,128)(2,1)}, u32[]{:S(2)}) copy-start(bf16[16,2048]{1,0:T(8,128)(2,1)} %param.21) | copy-start | bytes 196612
  7.2 87.4 %copy-start.7 = (bf16[128,2048]{1,0:T(8,128)(2,1)S(1)}, bf16[128,2048]{1,0:T(8,128)(2,1)}, u32[]{:S(2)}) copy-start(bf16[128,2048]{1,0:T(8,128)(2,1)} %param.16) | copy-start | bytes 1572868
  7.2 33.1 %all-gather.2.cloned.1.call-start = ((), (), s32[]{:S(2)}) async-start(), calls=%async_computation.2 | async-start | bytes 1310720 | tf_op jit(solution)/shard_map/all_gather | solution.py:41
  8.0 83.1 %all-reduce.3.cloned.1.call-start = ((), (), s32[]{:S(2)}) async-start(), calls=%async_computation.3 | async-start | bytes 2097152 | tf_op jit(solution)/shard_map/psum | solution.py:47
  55.3 75.7 %reduce-scatter.7.cloned.1.call-start = ((), (), s32[]{:S(2)}) async-start(), calls=%async_computation.6 | async-start | bytes 81920
  92.5 0.8 copy-start.2
  94.4 25.7 %copy-start.4 = (bf16[16,4096]{1,0:T(8,128)(2,1)S(1)}, bf16[16,4096]{1,0:T(8,128)(2,1)}, u32[]{:S(2)}) copy-start(bf16[16,4096]{1,0:T(8,128)(2,1)} %param.20) | copy-start | bytes 393220
  94.4 72.5 %reduce-scatter.5.cloned.1.call-start = ((), (), s32[]{:S(2)}) async-start(), calls=%async_computation.4 | async-start | bytes 2621440 | tf_op jit(solution)/shard_map/reduce_scatter | solution.py:65
  107.8 25.0 %copy-start.1 = (bf16[128,4096]{1,0:T(8,128)(2,1)S(1)}, bf16[128,4096]{1,0:T(8,128)(2,1)}, u32[]{:S(2)}) copy-start(bf16[128,4096]{1,0:T(8,128)(2,1)} %all-gather.2.cloned.1.call-done) | copy-start | bytes 3145732
  122.5 82.0 %all-reduce.5.cloned.1.call-start = ((), (), s32[]{:S(2)}) async-start(), calls=%async_computation.5 | async-start | bytes 524288 | tf_op jit(solution)/shard_map/psum | solution.py:71
Sparse Core Ops, SparseCore 0:
  9.6 30.6 all-gather.1
  55.4 35.5 all-reduce.2
  94.5 19.4 reduce-scatter.6
  122.6 44.2 reduce-scatter.4
  169.8 34.6 all-reduce.4
where the time goes:
time: 213 us
  waiting for transfers between devices  135 us (63%)
  matrix products  50.8 us (24%)
  between operations  13.9 us (7%)
  blocking collectives  6 us (3%)
  other arithmetic  3.28 us (2%)
  local copies, waits for them, and re-layouts  3.27 us (2%)
    dot_general x5, matrix products, contract_trailing(): lax.dot_general(left, right, (((1,), (1,)), ((), ())), preferred_element_...  39 us
    psum x1, waiting for transfers between devices, body(): up_entry_gradient = lax.psum(up_entry_term, 'row')  35.8 us
    psum x1, waiting for transfers between devices, body(): hidden_gradient, down_full = lax.psum((hidden_piece, down_piece), 'col')  35.7 us
    all_gather x1, waiting for transfers between devices, body(): lax.all_gather(output_gradient, 'row', axis=0, tiled=True)  32.3 us
    reduce_scatter x1, waiting for transfers between devices, body(): lax.psum_scatter(input_piece, 'row', scatter_dimension=0, tiled=True)  30.6 us
    psum x1, blocking collectives, body(): hidden_gradient, down_full = lax.psum((hidden_piece, down_piece), 'col')  6 us
  transfers between devices with their start and end apart: 5, of which 4 were waited for; matrix products, arithmetic and copies ran while one was open for 18% of the time, Pallas kernels for 0%

commit v1 on v0

--- a/solution.py
+++ b/solution.py
@@ -68,7 +68,10 @@
     up_entry_term = adapter_scale * contract_leading(
         upper_full, inputs.astype(jnp.float32), matmul_accuracy=highest_setting
     )
-    up_entry_gradient = lax.psum(up_entry_term, "row")
+    peers, up_entry_gradient = (lax.axis_size("row"), up_entry_term)
+    for far in [1 << k for k in range(peers.bit_length() - 1)]:
+        swap = [(i, i ^ far) for i in range(peers)]
+        up_entry_gradient = up_entry_gradient + lax.ppermute(up_entry_gradient, "row", swap)
     up_exit_gradient = adapter_scale * jnp.dot(
         up_adapter_activations, up_gradient, preferred_element_type=jnp.float32
     )

time: 213 us -> 188 us (0.88)
  waiting for transfers between devices: 135 us -> 110 us
    ppermute x0 -> x2, waiting for transfers between devices: none -> 41.5 us  [body(): lax.ppermute(up_entry_gradient, 'row', swap)]
    psum x1 -> x0, waiting for transfers between devices: 35.8 us -> none  [body(): up_entry_gradient = lax.psum(up_entry_term, 'row')]
    reduce_scatter x1, waiting for transfers between devices: 30.6 us -> 0.01 us  [body(): lax.psum_scatter(input_piece, 'row', scatter_dimension=0, tiled=True)]
  transfers between devices with their start and end apart: 5 -> 6, of which waited for: 4 -> 4; matrix products, arithmetic and copies ran while one was open for 18% -> 19% of each run, Pallas kernels for 0% -> 0%
where the time goes in v1:
time: 188 us
  waiting for transfers between devices  110 us (59%)
  matrix products  49.9 us (27%)
  between operations  13.9 us (7%)
  blocking collectives  6 us (3%)
  other arithmetic  4.04 us (2%)
  starting transfers between devices  2.26 us (1%)
    ppermute x2, waiting for transfers between devices, body(): lax.ppermute(up_entry_gradient, 'row', swap)  41.5 us
    dot_general x5, matrix products, contract_trailing(): lax.dot_general(left, right, (((1,), (1,)), ((), ())), preferred_element_...  39 us
    psum x1, waiting for transfers between devices, body(): hidden_gradient, down_full = lax.psum((hidden_piece, down_piece), 'col')  35.7 us
    all_gather x1, waiting for transfers between devices, body(): lax.all_gather(output_gradient, 'row', axis=0, tiled=True)  32.3 us
    psum x1, blocking collectives, body(): hidden_gradient, down_full = lax.psum((hidden_piece, down_piece), 'col')  6 us
  transfers between devices with their start and end apart: 6, of which 4 were waited for; matrix products, arithmetic and copies ran while one was open for 19% of the time, Pallas kernels for 0%

profile of v1, /device:TPU:0, one launch (start us, length us, event | category | flops | bytes accessed | tf_op | source)
XLA Modules:
  0.0 187.9 jit_solution(1550529962076423907)
XLA Ops:
  7.2 0.0 copy-start
  7.2 0.0 copy-start.5
  7.2 0.0 copy-start.3
  7.2 0.0 copy-start.6
  7.2 0.0 copy-start.7
  7.2 0.0 all-gather.2.cloned.1.call-start
  7.3 0.7 all-gather.2.cloned.1.call-update
  8.0 0.0 all-reduce.2.cloned.1.call-start
  8.0 32.3 %all-gather.2.cloned.1.call-done = bf16[128,4096]{1,0:T(8,128)(2,1)} async-done(((bf16[32,4096]{1,0:T(8,128)(2,1)}), bf16[128,4096]{1,0:T(8,128)(2,1)}) %all-gather.2.cloned.1.call-update) | async-done | bytes 1048592 | tf_op jit(solution)/shard_map/all_gather | solution.py:41
  40.3 1.6 fusion.21
  41.9 11.8 %fusion.20 = f32[128,2048]{1,0:T(8,128)S(1)} fusion(bf16[128,4096]{1,0:T(8,128)(2,1)} %all-gather.2.cloned.1.call-done, bf16[2048,4096]{1,0:T(8,128)(2,1)} %param.19), kind=kOutput, calls=%fused_computation.31 | convolution fusion | flops 2147483648 | bytes 18874368 | tf_op jit(solution)/shard_map/dot_general | solution.py:10
  53.7 0.0 copy-done.5
  53.7 1.6 fusion.1
  55.3 0.0 all-reduce.2.cloned.1.call-update
  55.3 0.0 reduce-scatter.7.cloned.1.call-start
  55.3 35.7 %all-reduce.2.cloned.1.call-done = f32[128,2048]{1,0:T(8,128)} async-done(((f32[128,2048]{1,0:T(8,128)}), f32[128,2048]{1,0:T(8,128)}) %all-reduce.2.cloned.1.call-update) | async-done | bytes 1048592 | tf_op jit(solution)/shard_map/psum | solution.py:47
  91.0 0.0 copy-done.3
  91.0 1.5 fusion.12
  92.5 0.0 copy-start.2
  92.5 0.8 copy-done.2
  93.3 0.0 copy-done.6
  93.3 0.2 fusion.22
  93.6 0.8 copy.18
  94.3 0.0 reduce-scatter.7.cloned.1.call-update
  94.4 0.0 copy-start.4
  94.4 0.2 reduce-scatter.5.cloned.1.call-start
  94.6 0.0 copy-done.7
  94.6 13.2 %fusion.13 = f32[128,4096]{1,0:T(8,128)} fusion(bf16[4096,2048]{1,0:T(8,128)(2,1)} %param.17, f32[128,2048]{1,0:T(8,128)} %all-reduce.2.cloned.1.call-done, bf16[128,2048]{1,0:T(8,128)(2,1)S(1)} %copy-done.7, bf16[128,2048]{1,0:T(8,128)(2,1)S(1)} %copy-done.3), kind=kOutput, calls=%fused_computation.26 | convolution fusion | flops 2150629376 | bytes 20971520 | tf_op jit(solution)/shard_map/dot_general | solution.py:10
  107.8 0.0 copy-start.1
  107.8 12.3 %convolution_add_fusion = f32[128,4096]{1,0:T(8,128)S(1)} fusion(f32[128,4096]{1,0:T(8,128)} %fusion.13, bf16[128,2048]{1,0:T(8,128)(2,1)} %copy-done.2, bf16[4096,2048]{1,0:T(8,128)(2,1)} %param.18), kind=kOutput, calls=%fused_computation.2 | convolution fusion | flops 2148007936 | bytes 21495808 | tf_op jit(solution)/shard_map/dot_general | solution.py:10
  120.1 0.0 copy-done.4
  120.1 2.4 %fusion = f32[128,4096]{1,0:T(8,128)} fusion(f32[128,4096]{1,0:T(8,128)S(1)} %convolution_add_fusion, f32[128,16]{0,1:T(8,128)S(1)} %fusion.22, bf16[16,4096]{1,0:T(8,128)(2,1)S(1)} %copy-done.4), kind=kOutput, calls=%fused_computation.1 | convolution fusion | flops 101711872 | bytes 4333568 | tf_op jit(solution)/shard_map/dot_general | solution.py:61
  122.5 0.0 reduce-scatter.5.cloned.1.call-update
  122.5 6.0 %psum.15 = bf16[128,16]{0,1:T(8,128)(2,1)S(1)} all-reduce(f32[128,16]{0,1:T(8,128)S(1)} %fusion.21), channel_id=1, replica_groups=mesh['grp'=2,'row'=4,'col'=4] {'col'}, use_global_device_ids=true, to_apply=%region_3.0 | all-reduce | flops 2048 | bytes 12288 | tf_op jit(solution)/shard_map/psum | solution.py:47
  128.5 0.0 reduce-scatter.7.cloned.1.call-done
  128.5 0.0 copy-done
  128.5 1.0 convolution_multiply_fusion.2
  129.6 1.6 collective-permute-start
  131.1 2.3 %convolution_multiply_fusion.5 = f32[16,2048]{1,0:T(8,128)} fusion(bf16[128,2048]{1,0:T(8,128)(2,1)} %param.16, bf16[128,2048]{1,0:T(8,128)(2,1)} %param.15, bf16[128,16]{0,1:T(8,128)(2,1)S(1)} %psum.15), kind=kOutput, calls=%fused_computation.9 | convolution fusion | flops 10518528 | bytes 1183744 | tf_op jit(solution)/shard_map/dot_general | solution.py:16
  133.4 15.9 %collective-permute-done = f32[16,4096]{1,0:T(8,128)S(1)} collective-permute-done((f32[16,4096]{1,0:T(8,128)S(1)}, f32[16,4096]{1,0:T(8,128)S(1)}, u32[]{:S(2)}, u32[]{:S(2)}) %collective-permute-start) | collective-permute-done | bytes 262176 | tf_op jit(solution)/shard_map/ppermute | solution.py:74
  149.3 0.4 collective-permute-start.1
  149.7 0.0 copy-done.1
  149.7 1.6 convolution_multiply_fusion.1
  151.3 1.9 %fusion.2 = f32[16,2048]{1,0:T(8,128)} fusion(bf16[16,128]{1,0:T(8,128)(2,1)} %param.24, bf16[128,2048]{1,0:T(8,128)(2,1)} %copy-done.2), kind=kOutput, calls=%fused_computation.8 | convolution fusion | flops 8421376 | bytes 659456 | tf_op jit(solution)/shard_map/dot_general | solution.py:75
  153.2 25.6 %collective-permute-done.1 = f32[16,4096]{1,0:T(8,128)S(1)} collective-permute-done((f32[16,4096]{1,0:T(8,128)S(1)}, f32[16,4096]{1,0:T(8,128)S(1)}, u32[]{:S(2)}, u32[]{:S(2)}) %collective-permute-start.1) | collective-permute-done | bytes 262176 | tf_op jit(solution)/shard_map/ppermute | solution.py:74
  178.9 0.7 add.35
  179.6 0.0 reduce-scatter.5.cloned.1.call-done
  179.6 1.8 convert_element_type.28
  (1 shorter events, 0.0 us)
Async XLA Ops:
  7.2 121.4 %copy-start = (bf16[32,4096]{1,0:T(8,128)(2,1)S(1)}, bf16[32,4096]{1,0:T(8,128)(2,1)}, u32[]{:S(2)}) copy-start(bf16[32,4096]{1,0:T(8,128)(2,1)} %param.13) | copy-start | bytes 786436
  7.2 46.5 %copy-start.5 = (bf16[16,2048]{1,0:T(8,128)(2,1)S(1)}, bf16[16,2048]{1,0:T(8,128)(2,1)}, u32[]{:S(2)}) copy-start(bf16[16,2048]{1,0:T(8,128)(2,1)} %param.22) | copy-start | bytes 196612
  7.2 83.8 %copy-start.3 = (bf16[128,2048]{1,0:T(8,128)(2,1)S(1)}, bf16[128,2048]{1,0:T(8,128)(2,1)}, u32[]{:S(2)}) copy-start(bf16[128,2048]{1,0:T(8,128)(2,1)} %param.15) | copy-start | bytes 1572868
  7.2 86.1 %copy-start.6 = (bf16[16,2048]{1,0:T(8,128)(2,1)S(1)}, bf16[16,2048]{1,0:T(8,128)(2,1)}, u32[]{:S(2)}) copy-start(bf16[16,2048]{1,0:T(8,128)(2,1)} %param.21) | copy-start | bytes 196612
  7.2 87.4 %copy-start.7 = (bf16[128,2048]{1,0:T(8,128)(2,1)S(1)}, bf16[128,2048]{1,0:T(8,128)(2,1)}, u32[]{:S(2)}) copy-start(bf16[128,2048]{1,0:T(8,128)(2,1)} %param.16) | copy-start | bytes 1572868
  7.2 33.1 %all-gather.2.cloned.1.call-start = ((), (), s32[]{:S(2)}) async-start(), calls=%async_computation.2 | async-start | bytes 1310720 | tf_op jit(solution)/shard_map/all_gather | solution.py:41
  8.0 83.1 %all-reduce.2.cloned.1.call-start = ((), (), s32[]{:S(2)}) async-start(), calls=%async_computation.3 | async-start | bytes 2097152 | tf_op jit(solution)/shard_map/psum | solution.py:47
  55.3 73.2 %reduce-scatter.7.cloned.1.call-start = ((), (), s32[]{:S(2)}) async-start(), calls=%async_computation.5 | async-start | bytes 81920
  92.5 0.8 copy-start.2
  94.4 25.7 %copy-start.4 = (bf16[16,4096]{1,0:T(8,128)(2,1)S(1)}, bf16[16,4096]{1,0:T(8,128)(2,1)}, u32[]{:S(2)}) copy-start(bf16[16,4096]{1,0:T(8,128)(2,1)} %param.20) | copy-start | bytes 393220
  94.4 85.2 %reduce-scatter.5.cloned.1.call-start = ((), (), s32[]{:S(2)}) async-start(), calls=%async_computation.4 | async-start | bytes 2621440 | tf_op jit(solution)/shard_map/reduce_scatter | solution.py:65
  107.8 41.9 %copy-start.1 = (bf16[128,4096]{1,0:T(8,128)(2,1)S(1)}, bf16[128,4096]{1,0:T(8,128)(2,1)}, u32[]{:S(2)}) copy-start(bf16[128,4096]{1,0:T(8,128)(2,1)} %all-gather.2.cloned.1.call-done) | copy-start | bytes 3145732
  129.6 19.7 %collective-permute-start = (f32[16,4096]{1,0:T(8,128)S(1)}, f32[16,4096]{1,0:T(8,128)S(1)}, u32[]{:S(2)}, u32[]{:S(2)}) collective-permute-start(f32[16,4096]{1,0:T(8,128)S(1)} %convolution_multiply_fusion.2), channel_id=1, source_target_pairs={{0,4},{4,0},{8,12},{12,8},{1,5},{5,1},{9,13},{13,9},{2,6},{6,2},{1... | collective-permute-start | bytes 786440 | tf_op jit(solution)/shard_map/ppermute | solution.py:74
  149.3 29.5 %collective-permute-start.1 = (f32[16,4096]{1,0:T(8,128)S(1)}, f32[16,4096]{1,0:T(8,128)S(1)}, u32[]{:S(2)}, u32[]{:S(2)}) collective-permute-start(f32[16,4096]{1,0:T(8,128)S(1)} %add.34), channel_id=1, source_target_pairs={{0,8},{4,12},{8,0},{12,4},{1,9},{5,13},{9,1},{13,5},{2,10},{6,14},... | collective-permute-start | bytes 786440 | tf_op jit(solution)/shard_map/ppermute | solution.py:74
Sparse Core Ops, SparseCore 0:
  9.6 30.6 all-gather.1
  55.4 35.5 all-reduce.1
  94.5 19.4 reduce-scatter.6
  122.6 55.2 reduce-scatter.4
